TPU v7x, 512 devices: a whole 4x4x16 slice. The times are simulated.
512 devices in a mesh: ad: 64 (over z, x), tp: 8 (over y, core).
Axes of the slice: x: 4, y: 4, z: 16, core: 2. Of those that a mesh axis runs over, the one named last changes fastest.
Arguments:
- tokens: bfloat16 [4, 3072, 8192], P(None, 'ad', 'tp'), may hold values from -6 to 6
- row_adapter_index: int32 [4, 3072], P(None, 'ad'), may hold values from 0 to 255, as said below
- key_base_weight: bfloat16 [8192, 1024], P('tp'), may hold values from -0.0625 to 0.0625
- adapter_down_weight: bfloat16 [256, 8192, 64], P('ad', 'tp'), may hold values from -0.0625 to 0.0625
- adapter_up_weight: bfloat16 [256, 64, 1024], P('ad', None, 'tp'), may hold values from -0.75 to 0.75
Outputs:
- token_keys_output: bfloat16 [4, 3072, 1024], P(None, 'ad', 'tp')
Inputs may be any that keep to these rules, and one draw needn't show every extreme that they name: `row_adapter_index`: group g holds adapters g * 4 to (g + 1) * 4 - 1. In each step the 48 rows of one index of ad name one group in exactly 2 rows and every other group in at most 1 row; that busiest group is the same for every index of ad in a step, so it receives 2 rows from each.
All inputs are finite; a program needn't handle non-finite values.
Results may differ from a plain program's by a relative error of at most 0.005.
Values may be sent and summed in bfloat16 or wider, within the bound.
A program may use at most 64 MiB of HBM per device.

v0:
```python
import jax
import jax.numpy as jnp
from jax import lax
from jax.sharding import PartitionSpec as P


def adapter_row_output(outgoing_rows, row_labels, down_weight_tile, up_weight_tile):
    adapter_number = down_weight_tile.shape[0]
    row_count = outgoing_rows.shape[0]
    down_all = jnp.einsum(
        "nd,adr->nar", outgoing_rows, down_weight_tile, preferred_element_type=jnp.float32
    )
    labels = (jnp.arange(adapter_number, dtype=jnp.int32) + 1).astype(jnp.bfloat16)
    selector = (row_labels[:, None] == labels[None, :]).astype(jnp.float32)
    down_part = jnp.sum(down_all * selector[:, :, None], axis=1)
    down_sum = lax.psum(down_part, "tp")
    down_low = down_sum.astype(jnp.bfloat16)
    spread_rows = (selector.astype(jnp.bfloat16)[:, :, None] * down_low[:, None, :]).reshape(
        row_count, -1
    )
    up_flat = up_weight_tile.reshape(
        adapter_number * up_weight_tile.shape[1], up_weight_tile.shape[2]
    )
    return jnp.dot(spread_rows, up_flat, preferred_element_type=jnp.float32).astype(jnp.bfloat16)


def body(tokens, row_adapter_index, key_base_weight, adapter_down_weight, adapter_up_weight):
    step_count, row_dev, width_per_shard = tokens.shape
    groups = lax.axis_size("ad")
    adapter_number = adapter_down_weight.shape[0]
    capacity = max(2, 3 * row_dev // groups)
    gathered_rows = tokens.reshape(step_count * row_dev, width_per_shard)
    partial_base = jnp.dot(gathered_rows, key_base_weight, preferred_element_type=jnp.float32)
    base_keys_output = lax.psum_scatter(partial_base, "tp", scatter_dimension=1, tiled=True)
    key_feature_width = base_keys_output.shape[1]
    outputs = []
    for step_index in range(step_count):
        step_rows = tokens[step_index]
        row_index_list = row_adapter_index[step_index]
        owner_group = row_index_list // adapter_number
        local_index = row_index_list % adapter_number
        group_hits = (owner_group[:, None] == jnp.arange(groups, dtype=jnp.int32)[None, :]).astype(
            jnp.int32
        )
        slot_rank = jnp.sum((jnp.cumsum(group_hits, axis=0) - group_hits) * group_hits, axis=1)
        tag_values = (local_index + 1).astype(jnp.float32)
        stays_remote = owner_group >= 0
        slot_index = jnp.where(stays_remote, owner_group * capacity + slot_rank, -1)
        dispatch = (
            slot_index[None, :] == jnp.arange(groups * capacity, dtype=jnp.int32)[:, None]
        ).astype(jnp.bfloat16)
        send_rows = jnp.dot(dispatch, step_rows, preferred_element_type=jnp.float32).astype(
            jnp.bfloat16
        )
        send_rows = send_rows.reshape(groups, capacity, width_per_shard)
        send_tags = (
            jnp.dot(dispatch.astype(jnp.float32), tag_values)
            .astype(jnp.bfloat16)
            .reshape(groups, capacity)
        )
        incoming_rows = lax.all_to_all(send_rows, "ad", split_axis=0, concat_axis=0, tiled=True)
        incoming_labels = lax.all_to_all(send_tags, "ad", split_axis=0, concat_axis=0, tiled=True)
        sender_number, slot_number = incoming_labels.shape
        adapter_update = adapter_row_output(
            incoming_rows.reshape(-1, width_per_shard),
            incoming_labels.reshape(-1),
            adapter_down_weight,
            adapter_up_weight,
        )
        adapter_update = adapter_update.reshape(sender_number, slot_number, key_feature_width)
        rows_sent_back = lax.all_to_all(
            adapter_update, "ad", split_axis=0, concat_axis=0, tiled=True
        )
        routed = jnp.dot(
            dispatch.T,
            rows_sent_back.reshape(groups * capacity, key_feature_width),
            preferred_element_type=jnp.float32,
        )
        step_base = base_keys_output[step_index * row_dev : (step_index + 1) * row_dev]
        outputs.append(step_base + routed)
    return jnp.stack(outputs).astype(jnp.bfloat16)


def solution(mesh):
    placed = (
        P(None, "ad", "tp"),
        P(None, "ad"),
        P("tp", None),
        P("ad", "tp", None),
        P("ad", None, "tp"),
    )
    return jax.shard_map(
        body, mesh=mesh, in_specs=placed, out_specs=P(None, "ad", "tp"), check_vma=False
    )
```

profile of v0, /device:TPU:2, one launch (start us, length us, event | category | flops | bytes accessed | tf_op | source)
XLA Modules:
  0.0 308.1 jit_solution(69769566374800532)
XLA Ops:
  6.5 0.9 and_select_fusion.10
  8.0 0.2 select_reduce_fusion.2
  8.2 0.2 select_reduce_fusion
  8.4 0.9 fusion.56
  9.4 0.8 all_to_all.67
  10.3 18.6 %all-to-all-start.9 = ((bf16[64,1,2]{2,1,0:T(2,128)(2,1)}), bf16[64,1,2]{2,1,0:T(2,128)(2,1)S(1)}, u32[]{:S(2)}, u32[]{:S(2)}) async-start(bf16[64,1,2]{2,1,0:T(2,128)(2,1)} %all_to_all.67), calls=%async_computation.10 | async-start | bytes 65536 | tf_op jit(solution)/shard_map/all_to_all | solution.py:62
  29.0 0.8 all_to_all.65
  29.9 12.9 %all-to-all-done.9 = bf16[64,1,2]{2,1,0:T(2,128)(2,1)S(1)} async-done(((bf16[64,1,2]{2,1,0:T(2,128)(2,1)}), bf16[64,1,2]{2,1,0:T(2,128)(2,1)S(1)}, u32[]{:S(2)}, u32[]{:S(2)}) %all-to-all-start.9) | async-done | bytes 288 | tf_op jit(solution)/shard_map/all_to_all | solution.py:62
  42.7 5.5 %all-to-all-start.3 = ((bf16[64,1,2]{2,1,0:T(2,128)(2,1)}), bf16[64,1,2]{2,1,0:T(2,128)(2,1)S(1)}, u32[]{:S(2)}, u32[]{:S(2)}) async-start(bf16[64,1,2]{2,1,0:T(2,128)(2,1)} %all_to_all.65), calls=%async_computation.4 | async-start | bytes 65536 | tf_op jit(solution)/shard_map/all_to_all | solution.py:62
  48.3 0.8 all_to_all.66
  49.1 12.7 %all-to-all-done.3 = bf16[64,1,2]{2,1,0:T(2,128)(2,1)S(1)} async-done(((bf16[64,1,2]{2,1,0:T(2,128)(2,1)}), bf16[64,1,2]{2,1,0:T(2,128)(2,1)S(1)}, u32[]{:S(2)}, u32[]{:S(2)}) %all-to-all-start.3) | async-done | bytes 288 | tf_op jit(solution)/shard_map/all_to_all | solution.py:62
  61.8 5.6 %all-to-all-start.6 = ((bf16[64,1,2]{2,1,0:T(2,128)(2,1)}), bf16[64,1,2]{2,1,0:T(2,128)(2,1)S(1)}, u32[]{:S(2)}, u32[]{:S(2)}) async-start(bf16[64,1,2]{2,1,0:T(2,128)(2,1)} %all_to_all.66), calls=%async_computation.7 | async-start | bytes 65536 | tf_op jit(solution)/shard_map/all_to_all | solution.py:62
  67.6 0.8 all_to_all.64
  68.4 12.9 %all-to-all-done.6 = bf16[64,1,2]{2,1,0:T(2,128)(2,1)S(1)} async-done(((bf16[64,1,2]{2,1,0:T(2,128)(2,1)}), bf16[64,1,2]{2,1,0:T(2,128)(2,1)S(1)}, u32[]{:S(2)}, u32[]{:S(2)}) %all-to-all-start.6) | async-done | bytes 288 | tf_op jit(solution)/shard_map/all_to_all | solution.py:62
  81.4 0.6 copy-done.5
  82.0 5.5 %all-to-all-start = ((bf16[64,1,2]{2,1,0:T(2,128)(2,1)}), bf16[64,1,2]{2,1,0:T(2,128)(2,1)S(1)}, u32[]{:S(2)}, u32[]{:S(2)}) async-start(bf16[64,1,2]{2,1,0:T(2,128)(2,1)} %all_to_all.64), calls=%async_computation.1 | async-start | bytes 65536 | tf_op jit(solution)/shard_map/all_to_all | solution.py:62
  87.5 1.1 convolution_convert_fusion.3
  88.6 0.8 reshape.453
  89.4 11.9 %all-to-all-done = bf16[64,1,2]{2,1,0:T(2,128)(2,1)S(1)} async-done(((bf16[64,1,2]{2,1,0:T(2,128)(2,1)}), bf16[64,1,2]{2,1,0:T(2,128)(2,1)S(1)}, u32[]{:S(2)}, u32[]{:S(2)}) %all-to-all-start) | async-done | bytes 288 | tf_op jit(solution)/shard_map/all_to_all | solution.py:62
  101.3 5.5 %all-to-all-start.1 = ((bf16[64,2,1024]{2,1,0:T(2,128)(2,1)}), bf16[64,2,1024]{2,1,0:T(2,128)(2,1)S(1)}, u32[]{:S(2)}, u32[]{:S(2)}) async-start(bf16[64,2,1024]{2,1,0:T(2,128)(2,1)} %reshape.453), calls=%async_computation.2 | async-start | bytes 524288 | tf_op jit(solution)/shard_map/all_to_all | solution.py:61
  106.8 0.2 convolution_convert_fusion.1
  107.0 0.8 reshape.461
  107.8 16.6 %all-to-all-done.1 = bf16[64,2,1024]{2,1,0:T(2,128)(2,1)S(1)} async-done(((bf16[64,2,1024]{2,1,0:T(2,128)(2,1)}), bf16[64,2,1024]{2,1,0:T(2,128)(2,1)S(1)}, u32[]{:S(2)}, u32[]{:S(2)}) %all-to-all-start.1) | async-done | bytes 262176 | tf_op jit(solution)/shard_map/all_to_all | solution.py:61
  124.5 5.7 %all-to-all-start.7 = ((bf16[64,2,1024]{2,1,0:T(2,128)(2,1)}), bf16[64,2,1024]{2,1,0:T(2,128)(2,1)S(1)}, u32[]{:S(2)}, u32[]{:S(2)}) async-start(bf16[64,2,1024]{2,1,0:T(2,128)(2,1)} %reshape.461), calls=%async_computation.8 | async-start | bytes 524288 | tf_op jit(solution)/shard_map/all_to_all | solution.py:61
  130.2 0.2 convolution_convert_fusion.2
  130.4 0.8 reshape.457
  131.2 16.9 %all-to-all-done.7 = bf16[64,2,1024]{2,1,0:T(2,128)(2,1)S(1)} async-done(((bf16[64,2,1024]{2,1,0:T(2,128)(2,1)}), bf16[64,2,1024]{2,1,0:T(2,128)(2,1)S(1)}, u32[]{:S(2)}, u32[]{:S(2)}) %all-to-all-start.7) | async-done | bytes 262176 | tf_op jit(solution)/shard_map/all_to_all | solution.py:61
  148.1 6.3 %all-to-all-start.4 = ((bf16[64,2,1024]{2,1,0:T(2,128)(2,1)}), bf16[64,2,1024]{2,1,0:T(2,128)(2,1)}, u32[]{:S(2)}, u32[]{:S(2)}) async-start(bf16[64,2,1024]{2,1,0:T(2,128)(2,1)} %reshape.457), calls=%async_computation.5 | async-start | bytes 524288 | tf_op jit(solution)/shard_map/all_to_all | solution.py:61
  154.4 1.5 fusion.100
  156.0 0.9 convolution_convert_fusion
  156.9 1.8 reshape.465
  158.6 0.9 reduce.3
  159.5 0.1 eq.243
  159.6 0.9 reduce.1
  160.7 0.9 reduce.2
  161.7 0.9 reduce
  162.7 0.7 fusion.52
  163.5 8.6 %all-to-all-done.4 = bf16[64,2,1024]{2,1,0:T(2,128)(2,1)} async-done(((bf16[64,2,1024]{2,1,0:T(2,128)(2,1)}), bf16[64,2,1024]{2,1,0:T(2,128)(2,1)}, u32[]{:S(2)}, u32[]{:S(2)}) %all-to-all-start.4) | async-done | bytes 262176 | tf_op jit(solution)/shard_map/all_to_all | solution.py:61
  172.1 6.6 %all-to-all-start.10 = ((bf16[64,2,1024]{2,1,0:T(2,128)(2,1)}), bf16[64,2,1024]{2,1,0:T(2,128)(2,1)S(1)}, u32[]{:S(2)}, u32[]{:S(2)}) async-start(bf16[64,2,1024]{2,1,0:T(2,128)(2,1)} %reshape.465), calls=%async_computation.11 | async-start | bytes 524288 | tf_op jit(solution)/shard_map/all_to_all | solution.py:61
  178.7 0.3 fusion.101
  179.0 0.6 multiply_reduce_fusion.3
  179.8 0.3 fusion.103
  180.2 1.1 reshape.458
  181.2 0.3 fusion.102
  181.6 15.0 %all-to-all-done.10 = bf16[64,2,1024]{2,1,0:T(2,128)(2,1)S(1)} async-done(((bf16[64,2,1024]{2,1,0:T(2,128)(2,1)}), bf16[64,2,1024]{2,1,0:T(2,128)(2,1)S(1)}, u32[]{:S(2)}, u32[]{:S(2)}) %all-to-all-start.10) | async-done | bytes 262176 | tf_op jit(solution)/shard_map/all_to_all | solution.py:61
  196.6 0.3 fusion.104
  197.0 25.0 %all-reduce.2 = (bf16[128,64]{0,1:T(8,128)(2,1)S(1)}, bf16[128,64]{0,1:T(8,128)(2,1)S(1)}, bf16[128,64]{0,1:T(8,128)(2,1)S(1)}, bf16[128,64]{0,1:T(8,128)(2,1)S(1)}) all-reduce(f32[128,64]{0,1:T(8,128)S(1)} %multiply_reduce_fusion, f32[128,64]{0,1:T(8,128)S(1)} %multiply_reduce_fusion.1, ...), channel_id=1, replica_groups=mesh['ad'=64,'tp'=8] {'tp'}, use_global_device_ids=true, to_apply=%region_16.17 | all-reduce | flops 32768 | bytes 196608 | tf_op jit(solution)/shard_map/psum | solution.py:16
  222.0 0.8 fusion.3
  222.8 5.5 %all-to-all-start.11 = ((bf16[64,2,128]{2,1,0:T(2,128)(2,1)}), bf16[64,2,128]{2,1,0:T(2,128)(2,1)S(1)}, u32[]{:S(2)}, u32[]{:S(2)}) async-start(bf16[64,2,128]{2,1,0:T(2,128)(2,1)} %bitcast.50), calls=%async_computation.12 | async-start | bytes 65536 | tf_op jit(solution)/shard_map/all_to_all | solution.py:71
  228.3 0.8 fusion.2
  229.1 12.9 %all-to-all-done.11 = bf16[64,2,128]{2,1,0:T(2,128)(2,1)S(1)} async-done(((bf16[64,2,128]{2,1,0:T(2,128)(2,1)}), bf16[64,2,128]{2,1,0:T(2,128)(2,1)S(1)}, u32[]{:S(2)}, u32[]{:S(2)}) %all-to-all-start.11) | async-done | bytes 32800 | tf_op jit(solution)/shard_map/all_to_all | solution.py:71
  242.0 5.2 %all-to-all-start.8 = ((bf16[64,2,128]{2,1,0:T(2,128)(2,1)}), bf16[64,2,128]{2,1,0:T(2,128)(2,1)S(1)}, u32[]{:S(2)}, u32[]{:S(2)}) async-start(bf16[64,2,128]{2,1,0:T(2,128)(2,1)} %bitcast.37), calls=%async_computation.9 | async-start | bytes 65536 | tf_op jit(solution)/shard_map/all_to_all | solution.py:71
  247.2 0.8 fusion.1
  248.1 13.1 %all-to-all-done.8 = bf16[64,2,128]{2,1,0:T(2,128)(2,1)S(1)} async-done(((bf16[64,2,128]{2,1,0:T(2,128)(2,1)}), bf16[64,2,128]{2,1,0:T(2,128)(2,1)S(1)}, u32[]{:S(2)}, u32[]{:S(2)}) %all-to-all-start.8) | async-done | bytes 32800 | tf_op jit(solution)/shard_map/all_to_all | solution.py:71
  261.1 5.5 %all-to-all-start.5 = ((bf16[64,2,128]{2,1,0:T(2,128)(2,1)}), bf16[64,2,128]{2,1,0:T(2,128)(2,1)S(1)}, u32[]{:S(2)}, u32[]{:S(2)}) async-start(bf16[64,2,128]{2,1,0:T(2,128)(2,1)} %bitcast.24), calls=%async_computation.6 | async-start | bytes 65536 | tf_op jit(solution)/shard_map/all_to_all | solution.py:71
  266.6 0.8 fusion
  267.4 0.9 fusion.8
  268.3 11.9 %all-to-all-done.5 = bf16[64,2,128]{2,1,0:T(2,128)(2,1)S(1)} async-done(((bf16[64,2,128]{2,1,0:T(2,128)(2,1)}), bf16[64,2,128]{2,1,0:T(2,128)(2,1)S(1)}, u32[]{:S(2)}, u32[]{:S(2)}) %all-to-all-start.5) | async-done | bytes 32800 | tf_op jit(solution)/shard_map/all_to_all | solution.py:71
  280.2 5.5 %all-to-all-start.2 = ((bf16[64,2,128]{2,1,0:T(2,128)(2,1)}), bf16[64,2,128]{2,1,0:T(2,128)(2,1)S(1)}, u32[]{:S(2)}, u32[]{:S(2)}) async-start(bf16[64,2,128]{2,1,0:T(2,128)(2,1)} %bitcast.11), calls=%async_computation.3 | async-start | bytes 65536 | tf_op jit(solution)/shard_map/all_to_all | solution.py:71
  285.8 0.9 fusion.9
  286.7 0.9 fusion.10
  287.7 12.0 %all-to-all-done.2 = bf16[64,2,128]{2,1,0:T(2,128)(2,1)S(1)} async-done(((bf16[64,2,128]{2,1,0:T(2,128)(2,1)}), bf16[64,2,128]{2,1,0:T(2,128)(2,1)S(1)}, u32[]{:S(2)}, u32[]{:S(2)}) %all-to-all-start.2) | async-done | bytes 32800 | tf_op jit(solution)/shard_map/all_to_all | solution.py:71
  299.7 0.9 fusion.11
  300.6 0.6 pad_maximum_fusion
  (66 shorter events, 2.1 us)
Async XLA Ops:
  6.5 147.9 %copy-start = (bf16[1024,1024]{1,0:T(8,128)(2,1)S(1)}, bf16[1024,1024]{1,0:T(8,128)(2,1)}, u32[]{:S(2)}) copy-start(bf16[1024,1024]{1,0:T(8,128)(2,1)} %param.7) | copy-start | bytes 6291460
  6.5 100.3 %copy-start.2 = (bf16[4,48,1024]{2,1,0:T(8,128)(2,1)S(1)}, bf16[4,48,1024]{2,1,0:T(8,128)(2,1)}, u32[]{:S(2)}) copy-start(bf16[4,48,1024]{2,1,0:T(8,128)(2,1)} %param.5) | copy-start | bytes 1179652
  9.3 121.9 %copy-start.8 = (s32[48]{0:T(128)}, s32[48]{0:T(128)S(1)}, u32[]{:S(2)}) copy-start(s32[48]{0:T(128)S(1)} %get-tuple-element.17) | copy-start | bytes 580
  9.3 121.9 %copy-start.10 = (s32[48]{0:T(128)}, s32[48]{0:T(128)S(1)}, u32[]{:S(2)}) copy-start(s32[48]{0:T(128)S(1)} %get-tuple-element.19) | copy-start | bytes 580
  9.3 121.9 %copy-start.12 = (s32[48]{0:T(128)}, s32[48]{0:T(128)S(1)}, u32[]{:S(2)}) copy-start(s32[48]{0:T(128)S(1)} %get-tuple-element.18) | copy-start | bytes 580
  9.3 146.6 %copy-start.14 = (s32[48]{0:T(128)}, s32[48]{0:T(128)S(1)}, u32[]{:S(2)}) copy-start(s32[48]{0:T(128)S(1)} %get-tuple-element.20) | copy-start | bytes 580
  10.3 32.5 %all-to-all-start.9 = ((bf16[64,1,2]{2,1,0:T(2,128)(2,1)}), bf16[64,1,2]{2,1,0:T(2,128)(2,1)S(1)}, u32[]{:S(2)}, u32[]{:S(2)}) async-start(bf16[64,1,2]{2,1,0:T(2,128)(2,1)} %all_to_all.67), calls=%async_computation.10 | async-start | bytes 65536 | tf_op jit(solution)/shard_map/all_to_all | solution.py:62
  42.7 38.6 %copy-start.3 = (bf16[64,1,2]{2,1,0:T(2,128)(2,1)}, bf16[64,1,2]{2,1,0:T(2,128)(2,1)S(1)}, u32[]{:S(2)}) copy-start(bf16[64,1,2]{2,1,0:T(2,128)(2,1)S(1)} %all-to-all-done.9) | copy-start | bytes 772
  42.7 19.1 %all-to-all-start.3 = ((bf16[64,1,2]{2,1,0:T(2,128)(2,1)}), bf16[64,1,2]{2,1,0:T(2,128)(2,1)S(1)}, u32[]{:S(2)}, u32[]{:S(2)}) async-start(bf16[64,1,2]{2,1,0:T(2,128)(2,1)} %all_to_all.65), calls=%async_computation.4 | async-start | bytes 65536 | tf_op jit(solution)/shard_map/all_to_all | solution.py:62
  61.8 19.5 %copy-start.4 = (bf16[64,1,2]{2,1,0:T(2,128)(2,1)}, bf16[64,1,2]{2,1,0:T(2,128)(2,1)S(1)}, u32[]{:S(2)}) copy-start(bf16[64,1,2]{2,1,0:T(2,128)(2,1)S(1)} %all-to-all-done.3) | copy-start | bytes 772
  61.8 19.5 %all-to-all-start.6 = ((bf16[64,1,2]{2,1,0:T(2,128)(2,1)}), bf16[64,1,2]{2,1,0:T(2,128)(2,1)S(1)}, u32[]{:S(2)}, u32[]{:S(2)}) async-start(bf16[64,1,2]{2,1,0:T(2,128)(2,1)} %all_to_all.66), calls=%async_computation.7 | async-start | bytes 65536 | tf_op jit(solution)/shard_map/all_to_all | solution.py:62
  81.4 0.6 copy-start.5
  82.0 19.3 %all-to-all-start = ((bf16[64,1,2]{2,1,0:T(2,128)(2,1)}), bf16[64,1,2]{2,1,0:T(2,128)(2,1)S(1)}, u32[]{:S(2)}, u32[]{:S(2)}) async-start(bf16[64,1,2]{2,1,0:T(2,128)(2,1)} %all_to_all.64), calls=%async_computation.1 | async-start | bytes 65536 | tf_op jit(solution)/shard_map/all_to_all | solution.py:62
  101.3 53.2 %copy-start.6 = (bf16[64,1,2]{2,1,0:T(2,128)(2,1)}, bf16[64,1,2]{2,1,0:T(2,128)(2,1)S(1)}, u32[]{:S(2)}) copy-start(bf16[64,1,2]{2,1,0:T(2,128)(2,1)S(1)} %all-to-all-done) | copy-start | bytes 772
  101.3 23.2 %all-to-all-start.1 = ((bf16[64,2,1024]{2,1,0:T(2,128)(2,1)}), bf16[64,2,1024]{2,1,0:T(2,128)(2,1)S(1)}, u32[]{:S(2)}, u32[]{:S(2)}) async-start(bf16[64,2,1024]{2,1,0:T(2,128)(2,1)} %reshape.453), calls=%async_computation.2 | async-start | bytes 524288 | tf_op jit(solution)/shard_map/all_to_all | solution.py:61
  124.5 23.7 %all-to-all-start.7 = ((bf16[64,2,1024]{2,1,0:T(2,128)(2,1)}), bf16[64,2,1024]{2,1,0:T(2,128)(2,1)S(1)}, u32[]{:S(2)}, u32[]{:S(2)}) async-start(bf16[64,2,1024]{2,1,0:T(2,128)(2,1)} %reshape.461), calls=%async_computation.8 | async-start | bytes 524288 | tf_op jit(solution)/shard_map/all_to_all | solution.py:61
  148.1 24.0 %all-to-all-start.4 = ((bf16[64,2,1024]{2,1,0:T(2,128)(2,1)}), bf16[64,2,1024]{2,1,0:T(2,128)(2,1)}, u32[]{:S(2)}, u32[]{:S(2)}) async-start(bf16[64,2,1024]{2,1,0:T(2,128)(2,1)} %reshape.457), calls=%async_computation.5 | async-start | bytes 524288 | tf_op jit(solution)/shard_map/all_to_all | solution.py:61
  154.4 113.0 %reduce-scatter.2.cloned.1.call-start = ((), (), s32[]{:S(2)}) async-start(), calls=%async_computation.13 | async-start | bytes 884736 | tf_op jit(solution)/shard_map/reduce_scatter | solution.py:34
  155.9 22.8 %copy-start.1 = (bf16[4,1024,64]{1,2,0:T(8,128)(2,1)S(1)}, bf16[4,1024,64]{1,2,0:T(8,128)(2,1)}, u32[]{:S(2)}) copy-start(bf16[4,1024,64]{1,2,0:T(8,128)(2,1)} %param.8) | copy-start | bytes 1572868
  172.1 24.4 %all-to-all-start.10 = ((bf16[64,2,1024]{2,1,0:T(2,128)(2,1)}), bf16[64,2,1024]{2,1,0:T(2,128)(2,1)S(1)}, u32[]{:S(2)}, u32[]{:S(2)}) async-start(bf16[64,2,1024]{2,1,0:T(2,128)(2,1)} %reshape.465), calls=%async_computation.11 | async-start | bytes 524288 | tf_op jit(solution)/shard_map/all_to_all | solution.py:61
  179.7 17.2 %copy-start.7 = (f32[128,64]{0,1:T(8,128)S(1)}, f32[128,64]{0,1:T(8,128)}, u32[]{:S(2)}) copy-start(f32[128,64]{0,1:T(8,128)} %multiply_reduce_fusion.3) | copy-start | bytes 98308
  179.7 42.2 %copy-start.19 = (bf16[128,4]{0,1:T(4,128)(2,1)S(1)}, bf16[128,4]{0,1:T(4,128)(2,1)}, u32[]{:S(2)}) copy-start(bf16[128,4]{0,1:T(4,128)(2,1)} %get-tuple-element.40) | copy-start | bytes 3076
  179.8 42.2 %copy-start.20 = (bf16[4,64,128]{2,1,0:T(8,128)(2,1)S(1)}, bf16[4,64,128]{2,1,0:T(8,128)(2,1)}, u32[]{:S(2)}) copy-start(bf16[4,64,128]{2,1,0:T(8,128)(2,1)} %param.9) | copy-start | bytes 196612
  180.1 48.2 %copy-start.18 = (bf16[128,4]{0,1:T(4,128)(2,1)S(1)}, bf16[128,4]{0,1:T(4,128)(2,1)}, u32[]{:S(2)}) copy-start(bf16[128,4]{0,1:T(4,128)(2,1)} %get-tuple-element.38) | copy-start | bytes 3076
  180.1 67.1 %copy-start.17 = (bf16[128,4]{0,1:T(4,128)(2,1)S(1)}, bf16[128,4]{0,1:T(4,128)(2,1)}, u32[]{:S(2)}) copy-start(bf16[128,4]{0,1:T(4,128)(2,1)} %get-tuple-element.36) | copy-start | bytes 3076
  180.1 86.5 %copy-start.16 = (bf16[128,4]{0,1:T(4,128)(2,1)S(1)}, bf16[128,4]{0,1:T(4,128)(2,1)}, u32[]{:S(2)}) copy-start(bf16[128,4]{0,1:T(4,128)(2,1)} %get-tuple-element.27) | copy-start | bytes 3076
  180.1 87.3 %copy-start.15 = (s32[48]{0:T(128)S(1)}, s32[48]{0:T(128)}, u32[]{:S(2)}) copy-start(s32[48]{0:T(128)} %copy-done.14) | copy-start | bytes 580
  180.1 105.6 %copy-start.13 = (s32[48]{0:T(128)S(1)}, s32[48]{0:T(128)}, u32[]{:S(2)}) copy-start(s32[48]{0:T(128)} %copy-done.12) | copy-start | bytes 580
  180.2 106.6 %copy-start.11 = (s32[48]{0:T(128)S(1)}, s32[48]{0:T(128)}, u32[]{:S(2)}) copy-start(s32[48]{0:T(128)} %copy-done.10) | copy-start | bytes 580
  180.2 119.5 %copy-start.9 = (s32[48]{0:T(128)S(1)}, s32[48]{0:T(128)}, u32[]{:S(2)}) copy-start(s32[48]{0:T(128)} %copy-done.8) | copy-start | bytes 580
  222.8 19.2 %all-to-all-start.11 = ((bf16[64,2,128]{2,1,0:T(2,128)(2,1)}), bf16[64,2,128]{2,1,0:T(2,128)(2,1)S(1)}, u32[]{:S(2)}, u32[]{:S(2)}) async-start(bf16[64,2,128]{2,1,0:T(2,128)(2,1)} %bitcast.50), calls=%async_computation.12 | async-start | bytes 65536 | tf_op jit(solution)/shard_map/all_to_all | solution.py:71
  242.0 19.1 %all-to-all-start.8 = ((bf16[64,2,128]{2,1,0:T(2,128)(2,1)}), bf16[64,2,128]{2,1,0:T(2,128)(2,1)S(1)}, u32[]{:S(2)}, u32[]{:S(2)}) async-start(bf16[64,2,128]{2,1,0:T(2,128)(2,1)} %bitcast.37), calls=%async_computation.9 | async-start | bytes 65536 | tf_op jit(solution)/shard_map/all_to_all | solution.py:71
  261.1 19.1 %all-to-all-start.5 = ((bf16[64,2,128]{2,1,0:T(2,128)(2,1)}), bf16[64,2,128]{2,1,0:T(2,128)(2,1)S(1)}, u32[]{:S(2)}, u32[]{:S(2)}) async-start(bf16[64,2,128]{2,1,0:T(2,128)(2,1)} %bitcast.24), calls=%async_computation.6 | async-start | bytes 65536 | tf_op jit(solution)/shard_map/all_to_all | solution.py:71
  280.2 19.4 %all-to-all-start.2 = ((bf16[64,2,128]{2,1,0:T(2,128)(2,1)}), bf16[64,2,128]{2,1,0:T(2,128)(2,1)S(1)}, u32[]{:S(2)}, u32[]{:S(2)}) async-start(bf16[64,2,128]{2,1,0:T(2,128)(2,1)} %bitcast.11), calls=%async_computation.3 | async-start | bytes 65536 | tf_op jit(solution)/shard_map/all_to_all | solution.py:71
Sparse Core Ops, SparseCore 0:
  158.0 40.8 reduce-scatter.1
where the time goes:
time: 309 us; the launch traced here: 308 us
  waiting for transfers between devices  157 us (51%)
  starting transfers between devices  81 us (26%)
  blocking collectives  25 us (8%)
  between operations  13.9 us (4%)
  matrix products  12.6 us (4%)
  local copies, waits for them, and re-layouts  10 us (3%)
  other arithmetic  8.13 us (3%)
    all_to_all x4, waiting for transfers between devices, body(): lax.all_to_all(send_rows, 'ad', split_axis=0, concat_axis=0, tiled=True)  57.2 us
    all_to_all x4, waiting for transfers between devices, body(): lax.all_to_all(send_tags, 'ad', split_axis=0, concat_axis=0, tiled=True)  50.4 us
    all_to_all x4, waiting for transfers between devices, body(): lax.all_to_all(adapter_update, 'ad', split_axis=0, concat_axis=0, tiled=T...  49.9 us
    all_to_all x4, starting transfers between devices, body(): lax.all_to_all(send_tags, 'ad', split_axis=0, concat_axis=0, tiled=True)  35.2 us
    psum x1, blocking collectives, adapter_row_output(): down_sum = lax.psum(down_part, 'tp')  25 us
    all_to_all x4, starting transfers between devices, body(): lax.all_to_all(send_rows, 'ad', split_axis=0, concat_axis=0, tiled=True)  24.1 us
    all_to_all x4, starting transfers between devices, body(): lax.all_to_all(adapter_update, 'ad', split_axis=0, concat_axis=0, tiled=T...  21.6 us
  transfers between devices with their start and end apart: 13, of which 12 were waited for; matrix products, arithmetic and copies ran while one was open for 7% of the time, Pallas kernels for 0%

commit v1 on v0

--- a/solution.py
+++ b/solution.py
@@ -2,6 +2,14 @@
 import jax.numpy as jnp
 from jax import lax
 from jax.sharding import PartitionSpec as P
+
+
+def doubling_sum(value, name):
+    size, total = (lax.axis_size(name), value)
+    for hop in [1 << k for k in range(size.bit_length() - 1)]:
+        swap = [(i, i ^ hop) for i in range(size)]
+        total = total + lax.ppermute(total, name, swap)
+    return total
 
 
 def adapter_row_output(outgoing_rows, row_labels, down_weight_tile, up_weight_tile):
@@ -13,7 +21,7 @@
     labels = (jnp.arange(adapter_number, dtype=jnp.int32) + 1).astype(jnp.bfloat16)
     selector = (row_labels[:, None] == labels[None, :]).astype(jnp.float32)
     down_part = jnp.sum(down_all * selector[:, :, None], axis=1)
-    down_sum = lax.psum(down_part, "tp")
+    down_sum = doubling_sum(down_part, "tp")
     down_low = down_sum.astype(jnp.bfloat16)
     spread_rows = (selector.astype(jnp.bfloat16)[:, :, None] * down_low[:, None, :]).reshape(
         row_count, -1

time: 309 us -> 320 us (1.036)
  the two profiles are of different devices: /device:TPU:2 before, /device:TPU:16 now
where the time goes in v1:
time: 320 us; the launch traced here: 318 us
  waiting for transfers between devices  164 us (51%)
  starting transfers between devices  107 us (33%)
  between operations  14.2 us (4%)
  matrix products  11.9 us (4%)
  local copies, waits for them, and re-layouts  11.7 us (4%)
  other arithmetic  9.01 us (3%)
    all_to_all x4, waiting for transfers between devices, body(): lax.all_to_all(send_rows, 'ad', split_axis=0, concat_axis=0, tiled=True)  56.6 us
    all_to_all x4, waiting for transfers between devices, body(): lax.all_to_all(send_tags, 'ad', split_axis=0, concat_axis=0, tiled=True)  54 us
    all_to_all x4, waiting for transfers between devices, body(): lax.all_to_all(adapter_update, 'ad', split_axis=0, concat_axis=0, tiled=T...  53.3 us
    ppermute x12, starting transfers between devices, doubling_sum(): total = total + lax.ppermute(total, name, swap)  34.7 us
    all_to_all x4, starting transfers between devices, body(): lax.all_to_all(send_tags, 'ad', split_axis=0, concat_axis=0, tiled=True)  32.2 us
    all_to_all x4, starting transfers between devices, body(): lax.all_to_all(send_rows, 'ad', split_axis=0, concat_axis=0, tiled=True)  20.2 us
    all_to_all x4, starting transfers between devices, body(): lax.all_to_all(adapter_update, 'ad', split_axis=0, concat_axis=0, tiled=T...  19.9 us
  transfers between devices with their start and end apart: 25, of which 12 were waited for; matrix products, arithmetic and copies ran while one was open for 7% of the time, Pallas kernels for 0%

profile of v1, /device:TPU:16, one launch (start us, length us, event | category | flops | bytes accessed | tf_op | source)
XLA Modules:
  0.0 317.7 jit_solution(8404462014916152015)
XLA Ops:
  6.5 0.9 and_select_fusion.10
  8.4 0.9 fusion.56
  9.4 0.8 all_to_all.64
  10.3 18.6 %all-to-all-start = ((bf16[64,1,2]{2,1,0:T(2,128)(2,1)}), bf16[64,1,2]{2,1,0:T(2,128)(2,1)S(1)}, u32[]{:S(2)}, u32[]{:S(2)}) async-start(bf16[64,1,2]{2,1,0:T(2,128)(2,1)} %all_to_all.64), calls=%async_computation.1 | async-start | bytes 65536 | tf_op jit(solution)/shard_map/all_to_all | solution.py:70
  29.0 0.8 all_to_all.65
  29.8 13.6 %all-to-all-done = bf16[64,1,2]{2,1,0:T(2,128)(2,1)S(1)} async-done(((bf16[64,1,2]{2,1,0:T(2,128)(2,1)}), bf16[64,1,2]{2,1,0:T(2,128)(2,1)S(1)}, u32[]{:S(2)}, u32[]{:S(2)}) %all-to-all-start) | async-done | bytes 288 | tf_op jit(solution)/shard_map/all_to_all | solution.py:70
  43.4 4.6 %all-to-all-start.3 = ((bf16[64,1,2]{2,1,0:T(2,128)(2,1)}), bf16[64,1,2]{2,1,0:T(2,128)(2,1)S(1)}, u32[]{:S(2)}, u32[]{:S(2)}) async-start(bf16[64,1,2]{2,1,0:T(2,128)(2,1)} %all_to_all.65), calls=%async_computation.4 | async-start | bytes 65536 | tf_op jit(solution)/shard_map/all_to_all | solution.py:70
  48.1 0.8 all_to_all.66
  48.9 13.9 %all-to-all-done.3 = bf16[64,1,2]{2,1,0:T(2,128)(2,1)S(1)} async-done(((bf16[64,1,2]{2,1,0:T(2,128)(2,1)}), bf16[64,1,2]{2,1,0:T(2,128)(2,1)S(1)}, u32[]{:S(2)}, u32[]{:S(2)}) %all-to-all-start.3) | async-done | bytes 288 | tf_op jit(solution)/shard_map/all_to_all | solution.py:70
  62.8 4.6 %all-to-all-start.6 = ((bf16[64,1,2]{2,1,0:T(2,128)(2,1)}), bf16[64,1,2]{2,1,0:T(2,128)(2,1)S(1)}, u32[]{:S(2)}, u32[]{:S(2)}) async-start(bf16[64,1,2]{2,1,0:T(2,128)(2,1)} %all_to_all.66), calls=%async_computation.7 | async-start | bytes 65536 | tf_op jit(solution)/shard_map/all_to_all | solution.py:70
  67.5 0.8 all_to_all.67
  68.3 13.6 %all-to-all-done.6 = bf16[64,1,2]{2,1,0:T(2,128)(2,1)S(1)} async-done(((bf16[64,1,2]{2,1,0:T(2,128)(2,1)}), bf16[64,1,2]{2,1,0:T(2,128)(2,1)S(1)}, u32[]{:S(2)}, u32[]{:S(2)}) %all-to-all-start.6) | async-done | bytes 288 | tf_op jit(solution)/shard_map/all_to_all | solution.py:70
  82.5 4.6 %all-to-all-start.9 = ((bf16[64,1,2]{2,1,0:T(2,128)(2,1)}), bf16[64,1,2]{2,1,0:T(2,128)(2,1)S(1)}, u32[]{:S(2)}, u32[]{:S(2)}) async-start(bf16[64,1,2]{2,1,0:T(2,128)(2,1)} %all_to_all.67), calls=%async_computation.10 | async-start | bytes 65536 | tf_op jit(solution)/shard_map/all_to_all | solution.py:70
  87.1 1.1 convolution_convert_fusion.3
  88.2 0.8 reshape.453
  89.0 12.9 %all-to-all-done.9 = bf16[64,1,2]{2,1,0:T(2,128)(2,1)S(1)} async-done(((bf16[64,1,2]{2,1,0:T(2,128)(2,1)}), bf16[64,1,2]{2,1,0:T(2,128)(2,1)S(1)}, u32[]{:S(2)}, u32[]{:S(2)}) %all-to-all-start.9) | async-done | bytes 288 | tf_op jit(solution)/shard_map/all_to_all | solution.py:70
  101.8 4.6 %all-to-all-start.1 = ((bf16[64,2,1024]{2,1,0:T(2,128)(2,1)}), bf16[64,2,1024]{2,1,0:T(2,128)(2,1)S(1)}, u32[]{:S(2)}, u32[]{:S(2)}) async-start(bf16[64,2,1024]{2,1,0:T(2,128)(2,1)} %reshape.453), calls=%async_computation.2 | async-start | bytes 524288 | tf_op jit(solution)/shard_map/all_to_all | solution.py:69
  106.7 0.8 reshape.457
  107.5 17.7 %all-to-all-done.1 = bf16[64,2,1024]{2,1,0:T(2,128)(2,1)S(1)} async-done(((bf16[64,2,1024]{2,1,0:T(2,128)(2,1)}), bf16[64,2,1024]{2,1,0:T(2,128)(2,1)S(1)}, u32[]{:S(2)}, u32[]{:S(2)}) %all-to-all-start.1) | async-done | bytes 262176 | tf_op jit(solution)/shard_map/all_to_all | solution.py:69
  125.9 4.6 %all-to-all-start.4 = ((bf16[64,2,1024]{2,1,0:T(2,128)(2,1)}), bf16[64,2,1024]{2,1,0:T(2,128)(2,1)S(1)}, u32[]{:S(2)}, u32[]{:S(2)}) async-start(bf16[64,2,1024]{2,1,0:T(2,128)(2,1)} %reshape.457), calls=%async_computation.5 | async-start | bytes 524288 | tf_op jit(solution)/shard_map/all_to_all | solution.py:69
  130.7 0.8 reshape.461
  131.5 17.7 %all-to-all-done.4 = bf16[64,2,1024]{2,1,0:T(2,128)(2,1)S(1)} async-done(((bf16[64,2,1024]{2,1,0:T(2,128)(2,1)}), bf16[64,2,1024]{2,1,0:T(2,128)(2,1)S(1)}, u32[]{:S(2)}, u32[]{:S(2)}) %all-to-all-start.4) | async-done | bytes 262176 | tf_op jit(solution)/shard_map/all_to_all | solution.py:69
  149.3 5.5 %all-to-all-start.7 = ((bf16[64,2,1024]{2,1,0:T(2,128)(2,1)}), bf16[64,2,1024]{2,1,0:T(2,128)(2,1)}, u32[]{:S(2)}, u32[]{:S(2)}) async-start(bf16[64,2,1024]{2,1,0:T(2,128)(2,1)} %reshape.461), calls=%async_computation.8 | async-start | bytes 524288 | tf_op jit(solution)/shard_map/all_to_all | solution.py:69
  155.0 0.8 reshape.465
  155.8 0.9 reduce
  156.8 0.9 reduce.1
  157.8 0.9 reduce.2
  158.8 0.9 reduce.3
  160.5 1.0 reshape.454
  161.5 11.8 %all-to-all-done.7 = bf16[64,2,1024]{2,1,0:T(2,128)(2,1)} async-done(((bf16[64,2,1024]{2,1,0:T(2,128)(2,1)}), bf16[64,2,1024]{2,1,0:T(2,128)(2,1)}, u32[]{:S(2)}, u32[]{:S(2)}) %all-to-all-start.7) | async-done | bytes 262176 | tf_op jit(solution)/shard_map/all_to_all | solution.py:69
  173.4 5.5 %all-to-all-start.10 = ((bf16[64,2,1024]{2,1,0:T(2,128)(2,1)}), bf16[64,2,1024]{2,1,0:T(2,128)(2,1)}, u32[]{:S(2)}, u32[]{:S(2)}) async-start(bf16[64,2,1024]{2,1,0:T(2,128)(2,1)} %reshape.465), calls=%async_computation.11 | async-start | bytes 524288 | tf_op jit(solution)/shard_map/all_to_all | solution.py:69
  179.8 1.9 collective-permute-start
  182.2 2.4 collective-permute-start.3
  184.6 1.0 reshape.462
  186.0 2.1 collective-permute-start.6
  188.1 9.4 %all-to-all-done.10 = bf16[64,2,1024]{2,1,0:T(2,128)(2,1)} async-done(((bf16[64,2,1024]{2,1,0:T(2,128)(2,1)}), bf16[64,2,1024]{2,1,0:T(2,128)(2,1)}, u32[]{:S(2)}, u32[]{:S(2)}) %all-to-all-start.10) | async-done | bytes 262176 | tf_op jit(solution)/shard_map/all_to_all | solution.py:69
  197.5 1.0 reshape.466
  198.9 1.9 collective-permute-start.9
  200.8 0.8 add.140
  201.6 3.2 %collective-permute-start.1 = (f32[128,64]{0,1:T(8,128)S(1)}, f32[128,64]{0,1:T(8,128)S(1)}, u32[]{:S(2)}, u32[]{:S(2)}) collective-permute-start(f32[128,64]{0,1:T(8,128)S(1)} %add.140), channel_id=1, source_target_pairs={{0,2},{1,3},{2,0},{3,1},{4,6},{5,7},{6,4},{7,5},{8,10},{9,11},{10,... | collective-permute-start | bytes 98312 | tf_op jit(solution)/shard_map/ppermute | solution.py:11
  204.8 2.7 collective-permute-start.4
  207.5 3.2 %collective-permute-start.7 = (f32[128,64]{0,1:T(8,128)S(1)}, f32[128,64]{0,1:T(8,128)S(1)}, u32[]{:S(2)}, u32[]{:S(2)}) collective-permute-start(f32[128,64]{0,1:T(8,128)S(1)} %add.154), channel_id=1, source_target_pairs={{0,2},{1,3},{2,0},{3,1},{4,6},{5,7},{6,4},{7,5},{8,10},{9,11},{10,... | collective-permute-start | bytes 98312 | tf_op jit(solution)/shard_map/ppermute | solution.py:11
  210.7 2.7 collective-permute-start.10
  213.4 2.2 collective-permute-start.2
  215.7 1.5 fusion.100
  217.3 5.1 %collective-permute-start.5 = (f32[128,64]{0,1:T(8,128)S(1)}, f32[128,64]{0,1:T(8,128)S(1)}, u32[]{:S(2)}, u32[]{:S(2)}) collective-permute-start(f32[128,64]{0,1:T(8,128)S(1)} %add.148), channel_id=1, source_target_pairs={{0,4},{1,5},{2,6},{3,7},{4,0},{5,1},{6,2},{7,3},{8,12},{9,13},{10,... | collective-permute-start | bytes 98312 | tf_op jit(solution)/shard_map/ppermute | solution.py:11
  222.4 2.2 collective-permute-start.8
  224.7 5.1 %collective-permute-start.11 = (f32[128,64]{0,1:T(8,128)S(1)}, f32[128,64]{0,1:T(8,128)S(1)}, u32[]{:S(2)}, u32[]{:S(2)}) collective-permute-start(f32[128,64]{0,1:T(8,128)S(1)} %add.162), channel_id=1, source_target_pairs={{0,4},{1,5},{2,6},{3,7},{4,0},{5,1},{6,2},{7,3},{8,12},{9,13},{10,... | collective-permute-start | bytes 98312 | tf_op jit(solution)/shard_map/ppermute | solution.py:11
  229.9 0.8 fusion
  230.7 6.1 %all-to-all-start.2 = ((bf16[64,2,128]{2,1,0:T(2,128)(2,1)}), bf16[64,2,128]{2,1,0:T(2,128)(2,1)S(1)}, u32[]{:S(2)}, u32[]{:S(2)}) async-start(bf16[64,2,128]{2,1,0:T(2,128)(2,1)} %bitcast.11), calls=%async_computation.3 | async-start | bytes 65536 | tf_op jit(solution)/shard_map/all_to_all | solution.py:79
  236.9 0.8 fusion.1
  237.7 0.8 fusion.2
  238.5 13.0 %all-to-all-done.2 = bf16[64,2,128]{2,1,0:T(2,128)(2,1)S(1)} async-done(((bf16[64,2,128]{2,1,0:T(2,128)(2,1)}), bf16[64,2,128]{2,1,0:T(2,128)(2,1)S(1)}, u32[]{:S(2)}, u32[]{:S(2)}) %all-to-all-start.2) | async-done | bytes 32800 | tf_op jit(solution)/shard_map/all_to_all | solution.py:79
  251.5 4.6 %all-to-all-start.5 = ((bf16[64,2,128]{2,1,0:T(2,128)(2,1)}), bf16[64,2,128]{2,1,0:T(2,128)(2,1)S(1)}, u32[]{:S(2)}, u32[]{:S(2)}) async-start(bf16[64,2,128]{2,1,0:T(2,128)(2,1)} %bitcast.24), calls=%async_computation.6 | async-start | bytes 65536 | tf_op jit(solution)/shard_map/all_to_all | solution.py:79
  256.2 14.7 %all-to-all-done.5 = bf16[64,2,128]{2,1,0:T(2,128)(2,1)S(1)} async-done(((bf16[64,2,128]{2,1,0:T(2,128)(2,1)}), bf16[64,2,128]{2,1,0:T(2,128)(2,1)S(1)}, u32[]{:S(2)}, u32[]{:S(2)}) %all-to-all-start.5) | async-done | bytes 32800 | tf_op jit(solution)/shard_map/all_to_all | solution.py:79
  270.9 4.6 %all-to-all-start.8 = ((bf16[64,2,128]{2,1,0:T(2,128)(2,1)}), bf16[64,2,128]{2,1,0:T(2,128)(2,1)S(1)}, u32[]{:S(2)}, u32[]{:S(2)}) async-start(bf16[64,2,128]{2,1,0:T(2,128)(2,1)} %bitcast.37), calls=%async_computation.9 | async-start | bytes 65536 | tf_op jit(solution)/shard_map/all_to_all | solution.py:79
  275.5 0.8 fusion.3
  276.3 0.9 fusion.11
  277.2 12.8 %all-to-all-done.8 = bf16[64,2,128]{2,1,0:T(2,128)(2,1)S(1)} async-done(((bf16[64,2,128]{2,1,0:T(2,128)(2,1)}), bf16[64,2,128]{2,1,0:T(2,128)(2,1)S(1)}, u32[]{:S(2)}, u32[]{:S(2)}) %all-to-all-start.8) | async-done | bytes 32800 | tf_op jit(solution)/shard_map/all_to_all | solution.py:79
  290.1 4.6 %all-to-all-start.11 = ((bf16[64,2,128]{2,1,0:T(2,128)(2,1)}), bf16[64,2,128]{2,1,0:T(2,128)(2,1)S(1)}, u32[]{:S(2)}, u32[]{:S(2)}) async-start(bf16[64,2,128]{2,1,0:T(2,128)(2,1)} %bitcast.50), calls=%async_computation.12 | async-start | bytes 65536 | tf_op jit(solution)/shard_map/all_to_all | solution.py:79
  294.7 0.9 fusion.10
  295.6 0.9 fusion.9
  296.6 12.8 %all-to-all-done.11 = bf16[64,2,128]{2,1,0:T(2,128)(2,1)S(1)} async-done(((bf16[64,2,128]{2,1,0:T(2,128)(2,1)}), bf16[64,2,128]{2,1,0:T(2,128)(2,1)S(1)}, u32[]{:S(2)}, u32[]{:S(2)}) %all-to-all-start.11) | async-done | bytes 32800 | tf_op jit(solution)/shard_map/all_to_all | solution.py:79
  309.3 0.9 fusion.8
  (101 shorter events, 7.6 us)
Async XLA Ops:
  6.5 209.1 %copy-start = (bf16[1024,1024]{1,0:T(8,128)(2,1)S(1)}, bf16[1024,1024]{1,0:T(8,128)(2,1)}, u32[]{:S(2)}) copy-start(bf16[1024,1024]{1,0:T(8,128)(2,1)} %param.7) | copy-start | bytes 6291460
  6.5 99.9 %copy-start.2 = (bf16[4,48,1024]{2,1,0:T(8,128)(2,1)S(1)}, bf16[4,48,1024]{2,1,0:T(8,128)(2,1)}, u32[]{:S(2)}) copy-start(bf16[4,48,1024]{2,1,0:T(8,128)(2,1)} %param.5) | copy-start | bytes 1179652
  9.3 97.4 %copy-start.12 = (s32[48]{0:T(128)}, s32[48]{0:T(128)S(1)}, u32[]{:S(2)}) copy-start(s32[48]{0:T(128)S(1)} %get-tuple-element.15) | copy-start | bytes 580
  9.3 97.4 %copy-start.14 = (s32[48]{0:T(128)}, s32[48]{0:T(128)S(1)}, u32[]{:S(2)}) copy-start(s32[48]{0:T(128)S(1)} %get-tuple-element.13) | copy-start | bytes 580
  9.3 122.3 %copy-start.10 = (s32[48]{0:T(128)}, s32[48]{0:T(128)S(1)}, u32[]{:S(2)}) copy-start(s32[48]{0:T(128)S(1)} %get-tuple-element.14) | copy-start | bytes 580
  9.3 145.4 %copy-start.8 = (s32[48]{0:T(128)}, s32[48]{0:T(128)S(1)}, u32[]{:S(2)}) copy-start(s32[48]{0:T(128)S(1)} %get-tuple-element.16) | copy-start | bytes 580
  10.3 33.1 %all-to-all-start = ((bf16[64,1,2]{2,1,0:T(2,128)(2,1)}), bf16[64,1,2]{2,1,0:T(2,128)(2,1)S(1)}, u32[]{:S(2)}, u32[]{:S(2)}) async-start(bf16[64,1,2]{2,1,0:T(2,128)(2,1)} %all_to_all.64), calls=%async_computation.1 | async-start | bytes 65536 | tf_op jit(solution)/shard_map/all_to_all | solution.py:70
  43.4 38.5 %copy-start.4 = (bf16[64,1,2]{2,1,0:T(2,128)(2,1)}, bf16[64,1,2]{2,1,0:T(2,128)(2,1)S(1)}, u32[]{:S(2)}) copy-start(bf16[64,1,2]{2,1,0:T(2,128)(2,1)S(1)} %all-to-all-done) | copy-start | bytes 772
  43.4 19.4 %all-to-all-start.3 = ((bf16[64,1,2]{2,1,0:T(2,128)(2,1)}), bf16[64,1,2]{2,1,0:T(2,128)(2,1)S(1)}, u32[]{:S(2)}, u32[]{:S(2)}) async-start(bf16[64,1,2]{2,1,0:T(2,128)(2,1)} %all_to_all.65), calls=%async_computation.4 | async-start | bytes 65536 | tf_op jit(solution)/shard_map/all_to_all | solution.py:70
  62.7 19.2 %copy-start.5 = (bf16[64,1,2]{2,1,0:T(2,128)(2,1)}, bf16[64,1,2]{2,1,0:T(2,128)(2,1)S(1)}, u32[]{:S(2)}) copy-start(bf16[64,1,2]{2,1,0:T(2,128)(2,1)S(1)} %all-to-all-done.3) | copy-start | bytes 772
  62.8 19.2 %all-to-all-start.6 = ((bf16[64,1,2]{2,1,0:T(2,128)(2,1)}), bf16[64,1,2]{2,1,0:T(2,128)(2,1)S(1)}, u32[]{:S(2)}, u32[]{:S(2)}) async-start(bf16[64,1,2]{2,1,0:T(2,128)(2,1)} %all_to_all.66), calls=%async_computation.7 | async-start | bytes 65536 | tf_op jit(solution)/shard_map/all_to_all | solution.py:70
  81.9 0.6 copy-start.6
  82.5 19.3 %all-to-all-start.9 = ((bf16[64,1,2]{2,1,0:T(2,128)(2,1)}), bf16[64,1,2]{2,1,0:T(2,128)(2,1)S(1)}, u32[]{:S(2)}, u32[]{:S(2)}) async-start(bf16[64,1,2]{2,1,0:T(2,128)(2,1)} %all_to_all.67), calls=%async_computation.10 | async-start | bytes 65536 | tf_op jit(solution)/shard_map/all_to_all | solution.py:70
  101.8 4.9 %copy-start.7 = (bf16[64,1,2]{2,1,0:T(2,128)(2,1)}, bf16[64,1,2]{2,1,0:T(2,128)(2,1)S(1)}, u32[]{:S(2)}) copy-start(bf16[64,1,2]{2,1,0:T(2,128)(2,1)S(1)} %all-to-all-done.9) | copy-start | bytes 772
  101.8 23.3 %all-to-all-start.1 = ((bf16[64,2,1024]{2,1,0:T(2,128)(2,1)}), bf16[64,2,1024]{2,1,0:T(2,128)(2,1)S(1)}, u32[]{:S(2)}, u32[]{:S(2)}) async-start(bf16[64,2,1024]{2,1,0:T(2,128)(2,1)} %reshape.453), calls=%async_computation.2 | async-start | bytes 524288 | tf_op jit(solution)/shard_map/all_to_all | solution.py:69
  107.5 71.4 %copy-start.1 = (bf16[4,1024,64]{1,2,0:T(8,128)(2,1)S(1)}, bf16[4,1024,64]{1,2,0:T(8,128)(2,1)}, u32[]{:S(2)}) copy-start(bf16[4,1024,64]{1,2,0:T(8,128)(2,1)} %param.8) | copy-start | bytes 1572868
  125.2 0.7 copy-start.3
  125.9 23.4 %all-to-all-start.4 = ((bf16[64,2,1024]{2,1,0:T(2,128)(2,1)}), bf16[64,2,1024]{2,1,0:T(2,128)(2,1)S(1)}, u32[]{:S(2)}, u32[]{:S(2)}) async-start(bf16[64,2,1024]{2,1,0:T(2,128)(2,1)} %reshape.457), calls=%async_computation.5 | async-start | bytes 524288 | tf_op jit(solution)/shard_map/all_to_all | solution.py:69
  149.3 24.1 %all-to-all-start.7 = ((bf16[64,2,1024]{2,1,0:T(2,128)(2,1)}), bf16[64,2,1024]{2,1,0:T(2,128)(2,1)}, u32[]{:S(2)}, u32[]{:S(2)}) async-start(bf16[64,2,1024]{2,1,0:T(2,128)(2,1)} %reshape.461), calls=%async_computation.8 | async-start | bytes 524288 | tf_op jit(solution)/shard_map/all_to_all | solution.py:69
  173.4 24.1 %all-to-all-start.10 = ((bf16[64,2,1024]{2,1,0:T(2,128)(2,1)}), bf16[64,2,1024]{2,1,0:T(2,128)(2,1)}, u32[]{:S(2)}, u32[]{:S(2)}) async-start(bf16[64,2,1024]{2,1,0:T(2,128)(2,1)} %reshape.465), calls=%async_computation.11 | async-start | bytes 524288 | tf_op jit(solution)/shard_map/all_to_all | solution.py:69
  178.8 97.5 %reduce-scatter.2.cloned.1.call-start = ((), (), s32[]{:S(2)}) async-start(), calls=%async_computation.13 | async-start | bytes 884736 | tf_op jit(solution)/shard_map/reduce_scatter | solution.py:42
  179.8 21.0 %collective-permute-start = (f32[128,64]{0,1:T(8,128)}, f32[128,64]{0,1:T(8,128)}, u32[]{:S(2)}, u32[]{:S(2)}) collective-permute-start(f32[128,64]{0,1:T(8,128)} %multiply_reduce_fusion.3), channel_id=1, source_target_pairs={{0,1},{1,0},{2,3},{3,2},{4,5},{5,4},{6,7},{7,6},{8,9},{9,8},{10,11... | collective-permute-start | bytes 98312 | tf_op jit(solution)/shard_map/ppermute | solution.py:11
  182.2 22.6 %collective-permute-start.3 = (f32[128,64]{0,1:T(8,128)S(1)}, f32[128,64]{0,1:T(8,128)S(1)}, u32[]{:S(2)}, u32[]{:S(2)}) collective-permute-start(f32[128,64]{0,1:T(8,128)S(1)} %multiply_reduce_fusion.2), channel_id=1, source_target_pairs={{0,1},{1,0},{2,3},{3,2},{4,5},{5,4},{6,7},{7,6},{8,9},{9,8},{10,11... | collective-permute-start | bytes 98312 | tf_op jit(solution)/shard_map/ppermute | solution.py:11
  186.0 21.5 %collective-permute-start.6 = (f32[128,64]{0,1:T(8,128)S(1)}, f32[128,64]{0,1:T(8,128)S(1)}, u32[]{:S(2)}, u32[]{:S(2)}) collective-permute-start(f32[128,64]{0,1:T(8,128)S(1)} %multiply_reduce_fusion.1), channel_id=1, source_target_pairs={{0,1},{1,0},{2,3},{3,2},{4,5},{5,4},{6,7},{7,6},{8,9},{9,8},{10,11... | collective-permute-start | bytes 98312 | tf_op jit(solution)/shard_map/ppermute | solution.py:11
  198.9 11.8 %collective-permute-start.9 = (f32[128,64]{0,1:T(8,128)S(1)}, f32[128,64]{0,1:T(8,128)S(1)}, u32[]{:S(2)}, u32[]{:S(2)}) collective-permute-start(f32[128,64]{0,1:T(8,128)S(1)} %multiply_reduce_fusion), channel_id=1, source_target_pairs={{0,1},{1,0},{2,3},{3,2},{4,5},{5,4},{6,7},{7,6},{8,9},{9,8},{10,11... | collective-permute-start | bytes 98312 | tf_op jit(solution)/shard_map/ppermute | solution.py:11
  201.6 11.8 %collective-permute-start.1 = (f32[128,64]{0,1:T(8,128)S(1)}, f32[128,64]{0,1:T(8,128)S(1)}, u32[]{:S(2)}, u32[]{:S(2)}) collective-permute-start(f32[128,64]{0,1:T(8,128)S(1)} %add.140), channel_id=1, source_target_pairs={{0,2},{1,3},{2,0},{3,1},{4,6},{5,7},{6,4},{7,5},{8,10},{9,11},{10,... | collective-permute-start | bytes 98312 | tf_op jit(solution)/shard_map/ppermute | solution.py:11
  204.8 12.5 %collective-permute-start.4 = (f32[128,64]{0,1:T(8,128)S(1)}, f32[128,64]{0,1:T(8,128)S(1)}, u32[]{:S(2)}, u32[]{:S(2)}) collective-permute-start(f32[128,64]{0,1:T(8,128)S(1)} %add.147), channel_id=1, source_target_pairs={{0,2},{1,3},{2,0},{3,1},{4,6},{5,7},{6,4},{7,5},{8,10},{9,11},{10,... | collective-permute-start | bytes 98312 | tf_op jit(solution)/shard_map/ppermute | solution.py:11
  207.5 14.9 %collective-permute-start.7 = (f32[128,64]{0,1:T(8,128)S(1)}, f32[128,64]{0,1:T(8,128)S(1)}, u32[]{:S(2)}, u32[]{:S(2)}) collective-permute-start(f32[128,64]{0,1:T(8,128)S(1)} %add.154), channel_id=1, source_target_pairs={{0,2},{1,3},{2,0},{3,1},{4,6},{5,7},{6,4},{7,5},{8,10},{9,11},{10,... | collective-permute-start | bytes 98312 | tf_op jit(solution)/shard_map/ppermute | solution.py:11
  210.7 14.0 %collective-permute-start.10 = (f32[128,64]{0,1:T(8,128)S(1)}, f32[128,64]{0,1:T(8,128)S(1)}, u32[]{:S(2)}, u32[]{:S(2)}) collective-permute-start(f32[128,64]{0,1:T(8,128)S(1)} %add.161), channel_id=1, source_target_pairs={{0,2},{1,3},{2,0},{3,1},{4,6},{5,7},{6,4},{7,5},{8,10},{9,11},{10,... | collective-permute-start | bytes 98312 | tf_op jit(solution)/shard_map/ppermute | solution.py:11
  213.4 16.4 %collective-permute-start.2 = (f32[128,64]{0,1:T(8,128)S(1)}, f32[128,64]{0,1:T(8,128)S(1)}, u32[]{:S(2)}, u32[]{:S(2)}) collective-permute-start(f32[128,64]{0,1:T(8,128)S(1)} %add.141), channel_id=1, source_target_pairs={{0,4},{1,5},{2,6},{3,7},{4,0},{5,1},{6,2},{7,3},{8,12},{9,13},{10,... | collective-permute-start | bytes 98312 | tf_op jit(solution)/shard_map/ppermute | solution.py:11
  215.6 14.2 %copy-start.19 = (bf16[128,4]{0,1:T(4,128)(2,1)S(1)}, bf16[128,4]{0,1:T(4,128)(2,1)}, u32[]{:S(2)}) copy-start(bf16[128,4]{0,1:T(4,128)(2,1)} %get-tuple-element.23) | copy-start | bytes 3076
  215.7 14.2 %copy-start.20 = (bf16[4,64,128]{2,1,0:T(8,128)(2,1)S(1)}, bf16[4,64,128]{2,1,0:T(8,128)(2,1)}, u32[]{:S(2)}) copy-start(bf16[4,64,128]{2,1,0:T(8,128)(2,1)} %param.9) | copy-start | bytes 196612
  215.7 21.2 %copy-start.18 = (bf16[128,4]{0,1:T(4,128)(2,1)S(1)}, bf16[128,4]{0,1:T(4,128)(2,1)}, u32[]{:S(2)}) copy-start(bf16[128,4]{0,1:T(4,128)(2,1)} %get-tuple-element.32) | copy-start | bytes 3076
  215.7 22.0 %copy-start.17 = (bf16[128,4]{0,1:T(4,128)(2,1)S(1)}, bf16[128,4]{0,1:T(4,128)(2,1)}, u32[]{:S(2)}) copy-start(bf16[128,4]{0,1:T(4,128)(2,1)} %get-tuple-element.34) | copy-start | bytes 3076
  215.7 59.8 %copy-start.16 = (bf16[128,4]{0,1:T(4,128)(2,1)S(1)}, bf16[128,4]{0,1:T(4,128)(2,1)}, u32[]{:S(2)}) copy-start(bf16[128,4]{0,1:T(4,128)(2,1)} %get-tuple-element.36) | copy-start | bytes 3076
  215.7 60.6 %copy-start.15 = (s32[48]{0:T(128)S(1)}, s32[48]{0:T(128)}, u32[]{:S(2)}) copy-start(s32[48]{0:T(128)} %copy-done.14) | copy-start | bytes 580
  215.7 79.0 %copy-start.13 = (s32[48]{0:T(128)S(1)}, s32[48]{0:T(128)}, u32[]{:S(2)}) copy-start(s32[48]{0:T(128)} %copy-done.12) | copy-start | bytes 580
  215.7 79.9 %copy-start.11 = (s32[48]{0:T(128)S(1)}, s32[48]{0:T(128)}, u32[]{:S(2)}) copy-start(s32[48]{0:T(128)} %copy-done.10) | copy-start | bytes 580
  215.7 93.6 %copy-start.9 = (s32[48]{0:T(128)S(1)}, s32[48]{0:T(128)}, u32[]{:S(2)}) copy-start(s32[48]{0:T(128)} %copy-done.8) | copy-start | bytes 580
  217.3 19.5 %collective-permute-start.5 = (f32[128,64]{0,1:T(8,128)S(1)}, f32[128,64]{0,1:T(8,128)S(1)}, u32[]{:S(2)}, u32[]{:S(2)}) collective-permute-start(f32[128,64]{0,1:T(8,128)S(1)} %add.148), channel_id=1, source_target_pairs={{0,4},{1,5},{2,6},{3,7},{4,0},{5,1},{6,2},{7,3},{8,12},{9,13},{10,... | collective-permute-start | bytes 98312 | tf_op jit(solution)/shard_map/ppermute | solution.py:11
  222.4 14.4 %collective-permute-start.8 = (f32[128,64]{0,1:T(8,128)S(1)}, f32[128,64]{0,1:T(8,128)S(1)}, u32[]{:S(2)}, u32[]{:S(2)}) collective-permute-start(f32[128,64]{0,1:T(8,128)S(1)} %add.155), channel_id=1, source_target_pairs={{0,4},{1,5},{2,6},{3,7},{4,0},{5,1},{6,2},{7,3},{8,12},{9,13},{10,... | collective-permute-start | bytes 98312 | tf_op jit(solution)/shard_map/ppermute | solution.py:11
  224.7 31.4 %collective-permute-start.11 = (f32[128,64]{0,1:T(8,128)S(1)}, f32[128,64]{0,1:T(8,128)S(1)}, u32[]{:S(2)}, u32[]{:S(2)}) collective-permute-start(f32[128,64]{0,1:T(8,128)S(1)} %add.162), channel_id=1, source_target_pairs={{0,4},{1,5},{2,6},{3,7},{4,0},{5,1},{6,2},{7,3},{8,12},{9,13},{10,... | collective-permute-start | bytes 98312 | tf_op jit(solution)/shard_map/ppermute | solution.py:11
  230.7 20.9 %all-to-all-start.2 = ((bf16[64,2,128]{2,1,0:T(2,128)(2,1)}), bf16[64,2,128]{2,1,0:T(2,128)(2,1)S(1)}, u32[]{:S(2)}, u32[]{:S(2)}) async-start(bf16[64,2,128]{2,1,0:T(2,128)(2,1)} %bitcast.11), calls=%async_computation.3 | async-start | bytes 65536 | tf_op jit(solution)/shard_map/all_to_all | solution.py:79
  251.5 19.3 %all-to-all-start.5 = ((bf16[64,2,128]{2,1,0:T(2,128)(2,1)}), bf16[64,2,128]{2,1,0:T(2,128)(2,1)S(1)}, u32[]{:S(2)}, u32[]{:S(2)}) async-start(bf16[64,2,128]{2,1,0:T(2,128)(2,1)} %bitcast.24), calls=%async_computation.6 | async-start | bytes 65536 | tf_op jit(solution)/shard_map/all_to_all | solution.py:79
  270.9 19.2 %all-to-all-start.8 = ((bf16[64,2,128]{2,1,0:T(2,128)(2,1)}), bf16[64,2,128]{2,1,0:T(2,128)(2,1)S(1)}, u32[]{:S(2)}, u32[]{:S(2)}) async-start(bf16[64,2,128]{2,1,0:T(2,128)(2,1)} %bitcast.37), calls=%async_computation.9 | async-start | bytes 65536 | tf_op jit(solution)/shard_map/all_to_all | solution.py:79
  290.1 19.3 %all-to-all-start.11 = ((bf16[64,2,128]{2,1,0:T(2,128)(2,1)}), bf16[64,2,128]{2,1,0:T(2,128)(2,1)S(1)}, u32[]{:S(2)}, u32[]{:S(2)}) async-start(bf16[64,2,128]{2,1,0:T(2,128)(2,1)} %bitcast.50), calls=%async_computation.12 | async-start | bytes 65536 | tf_op jit(solution)/shard_map/all_to_all | solution.py:79
Sparse Core Ops, SparseCore 0:
  217.4 27.3 reduce-scatter.1
